TPU v7x, 32 devices: a whole 2x2x4 slice. The times are simulated.
32 devices in a mesh: tile: 4 (over y, x), mom: 2 (over core), ewin: 4 (over z).
Axes of the slice: x: 2, y: 2, z: 4, core: 2. Of those that a mesh axis runs over, the one named last changes fastest.
Arguments:
- green_ret: bfloat16 [2, 4, 4, 512, 1024], P('mom', 'ewin', 'tile'), may hold values from -0.25 to 0.25
- injection: float32 [2, 4, 4, 512], P('mom', 'ewin', 'tile'), may hold values from 0.1 to 1
- mom_shift: int32 [4], replicated, may hold values from 0 to 7, as said below
- phon_off: int32 [8], replicated, may hold values from -4 to 4
- coupling: float32 [4, 8], replicated, may hold values from 0.05 to 1
- tile_nbr: int32 [4, 4], replicated, may hold values from 0 to 3
Outputs:
- sigma_less: bfloat16 [2, 4, 4, 512, 1024], P('mom', 'ewin', None, 'tile')
Inputs may be any that keep to these rules, and one draw needn't show every extreme that they name: `mom_shift`: every residue from 0 to 1 appears among the 4 shifts taken modulo 2.
All inputs are finite; a program needn't handle non-finite values.
Results may differ from a plain program's by a relative error of at most 0.0036.
Values may be sent and summed in bfloat16 or wider, within the bound.
A program may use at most 64 MiB of HBM per device.

v0:
```python
import jax
import jax.numpy as jnp
from jax import lax
from jax.sharding import PartitionSpec as P

HW = 4
NW = 8


def with_halo(shard, sides, width):
    for axis, dim in sides:
        peers, length = (lax.axis_size(axis), shard.shape[dim])
        up = [(i, (i + 1) % peers) for i in range(peers - 1)]
        down = [(j, i) for i, j in up]
        last = lax.slice_in_dim(shard, length - width, length, axis=dim)
        initial = lax.slice_in_dim(shard, 0, width, axis=dim)
        before = lax.ppermute(last, axis, up)
        after = lax.ppermute(initial, axis, down)
        shard = jnp.concatenate([before, shard, after], axis=dim)
    return shard


def on_device(green_ret, injection, mom_shift, phon_off, coupling, tile_nbr):
    blocks = green_ret[0, 0]
    gamma = injection[0, 0]
    orbitals = blocks.shape[1]
    ntiles = lax.axis_size("tile")
    per_tile = orbitals // ntiles
    real_part = blocks[:, :, :orbitals].astype(jnp.float32)
    imag_part = blocks[:, :, orbitals:].astype(jnp.float32)
    scale = gamma[:, None, :]
    left_re = jnp.concatenate([real_part * scale, imag_part * scale], axis=2).astype(jnp.bfloat16)
    left_im = jnp.concatenate([imag_part * scale, -real_part * scale], axis=2).astype(jnp.bfloat16)
    real_out = jnp.einsum("prk,pck->prc", left_re, blocks, preferred_element_type=jnp.float32)
    imag_out = jnp.einsum("prk,pck->prc", left_im, blocks, preferred_element_type=jnp.float32)
    payload = jnp.concatenate([real_out, imag_out], axis=2).astype(jnp.bfloat16)
    exchanged = lax.all_to_all(payload, "tile", split_axis=1, concat_axis=0, tiled=True)
    energies = exchanged.shape[0]
    rimmed = with_halo(exchanged, (("ewin", 0),), HW)
    extended = lax.all_gather(rimmed[None], "mom", axis=0, tiled=True)
    nmom = lax.axis_size("mom")
    here = lax.axis_index("mom")
    source = jnp.mod(here - mom_shift, nmom)
    onehot = (source[:, None] == jnp.arange(nmom, dtype=jnp.int32)[None, :]).astype(jnp.float32)
    weights = jnp.dot(onehot.T, coupling, precision=lax.Precision.HIGHEST)
    total = jnp.zeros(exchanged.shape, jnp.float32)
    for offset in range(NW):
        start = HW + phon_off[offset]
        piece = lax.dynamic_slice_in_dim(extended, start, energies, 1)
        for moment in range(nmom):
            total = total + weights[moment, offset] * piece[moment].astype(jnp.float32)
    tile_here = lax.axis_index("tile")
    neighbours = lax.dynamic_index_in_dim(tile_nbr, tile_here, 0, keepdims=False)
    coltile = jnp.arange(orbitals, dtype=jnp.int32) // per_tile
    colmask = jnp.any(coltile[:, None] == neighbours[None, :], axis=1).astype(jnp.float32)
    colmask = jnp.concatenate([colmask, colmask])
    result = (total * colmask[None, None, :]).astype(jnp.bfloat16)
    return result[None, None]


def solution(mesh):
    placed = (
        P("mom", "ewin", "tile", None, None),
        P("mom", "ewin", "tile", None),
        P(),
        P(),
        P(),
        P(),
    )
    return jax.shard_map(
        on_device,
        mesh=mesh,
        in_specs=placed,
        out_specs=P("mom", "ewin", None, "tile", None),
        check_vma=False,
    )
```

profile of v0, /device:TPU:0, one launch (start us, length us, event | category | flops | bytes accessed | tf_op | source)
XLA Modules:
  0.0 113.0 jit_solution(7186449994337882947)
XLA Ops:
  6.5 0.0 copy-start
  6.5 0.0 copy-start.1
  6.5 0.0 all-gather.3.cloned.1.call-start
  6.5 1.6 %fusion.17 = (bf16[512,512]{1,0:T(8,128)(2,1)S(1)}, bf16[512,512]{1,0:T(8,128)(2,1)S(1)}, bf16[512,512]{1,0:T(8,128)(2,1)S(1)}) fusion(f32[512]{0:T(512)} %bitcast.71, bf16[1,512,1024]{2,1,0:T(8,128)(2,1)} %bitcast.70), kind=kLoop, calls=%fused_computation.25 | loop fusion | flops 2359296 | bytes 2623488 | tf_op jit(solution)/shard_map/concatenate | solution.py:32
  8.2 0.0 copy-done.1
  8.2 0.7 fusion.2
  8.9 0.7 fusion.3
  9.7 0.1 pad_maximum_fusion.1
  9.8 2.0 %copy.10 = bf16[1,512,1024]{2,0,1:T(2,128)(2,1)S(1)} copy(bf16[1,512,1024]{1,2,0:T(8,128)(2,1)S(1)} %pad_maximum_fusion.1) | data formatting | bytes 2097152 | tf_op jit(solution)/shard_map/concatenate | solution.py:36
  11.7 0.5 broadcast.191
  12.3 7.3 %reduce = bf16[512,1024]{1,0:T(8,128)(2,1)S(1)} reduce(bf16[512,1,1024]{2,1,0:T(2,128)(2,1)S(1)} %bitcast.66, bf16[]{:T(256)} %broadcast.191), dimensions={1}, to_apply=%bitcast.61.reduce_sub_computation | reduce | bytes 2097154
  19.6 0.8 reshape.449
  20.4 19.1 %all_to_all.12 = bf16[4,2,65536]{2,1,0:T(2,128)(2,1)S(1)} all-to-all(bf16[4,2,65536]{2,1,0:T(2,128)(2,1)S(1)} %reshape.449), channel_id=1, replica_groups=mesh['tile'=4,'mom'=2,'ewin'=4] {'tile'}, dimensions={0} | all-to-all | bytes 2097152 | tf_op jit(solution)/shard_map/all_to_all | solution.py:37
  39.5 0.9 reshape.450
  40.5 0.4 copy.11
  40.9 3.5 %collective-permute-start = (bf16[4,128,1024]{2,1,0:T(8,128)(2,1)S(1)}, bf16[4,128,1024]{2,1,0:T(8,128)(2,1)S(1)}, u32[]{:S(2)}, u32[]{:S(2)}) collective-permute-start(bf16[4,128,1024]{2,1,0:T(8,128)(2,1)S(1)} %bitcast.67), channel_id=1, source_target_pairs={{0,1},{1,2},{2,3},{4,5},{5,6},{6,7},{8,9},{9,10},{10,11},{12,13},{... | collective-permute-start | bytes 3145736 | tf_op jit(solution)/shard_map/ppermute | solution.py:17
  44.4 1.5 %collective-permute-start.1 = (bf16[4,128,1024]{2,1,0:T(8,128)(2,1)S(1)}, bf16[4,128,1024]{2,1,0:T(8,128)(2,1)S(1)}, u32[]{:S(2)}, u32[]{:S(2)}) collective-permute-start(bf16[4,128,1024]{2,1,0:T(8,128)(2,1)S(1)} %bitcast.68), channel_id=1, source_target_pairs={{1,0},{2,1},{3,2},{5,4},{6,5},{7,6},{9,8},{10,9},{11,10},{13,12},{... | collective-permute-start | bytes 3145736 | tf_op jit(solution)/shard_map/ppermute | solution.py:18
  45.9 19.4 %collective-permute-done = bf16[4,128,1024]{2,1,0:T(8,128)(2,1)S(1)} collective-permute-done((bf16[4,128,1024]{2,1,0:T(8,128)(2,1)S(1)}, bf16[4,128,1024]{2,1,0:T(8,128)(2,1)S(1)}, u32[]{:S(2)}, u32[]{:S(2)}) %collective-permute-start) | collective-permute-done | bytes 1048608 | tf_op jit(solution)/shard_map/ppermute | solution.py:17
  65.2 4.2 %collective-permute-done.1 = bf16[4,128,1024]{2,1,0:T(8,128)(2,1)S(1)} collective-permute-done((bf16[4,128,1024]{2,1,0:T(8,128)(2,1)S(1)}, bf16[4,128,1024]{2,1,0:T(8,128)(2,1)S(1)}, u32[]{:S(2)}, u32[]{:S(2)}) %collective-permute-start.1) | collective-permute-done | bytes 1048608 | tf_op jit(solution)/shard_map/ppermute | solution.py:18
  69.4 1.8 %pad_maximum_fusion = bf16[12,128,1024]{2,1,0:T(8,128)(2,1)} fusion(bf16[4,128,1024]{2,1,0:T(8,128)(2,1)S(1)} %collective-permute-done.1, bf16[4,128,1024]{2,1,0:T(8,128)(2,1)S(1)} %bitcast.69, bf16[4,128,1024]{2,1,0:T(8,128)(2,1)S(1)} %collective-permute-done), kind=kLoop, calls=%fused_computation | loop fusion | flops 3145728 | bytes 6291456 | tf_op jit(solution)/shard_map/concatenate | solution.py:19
  71.3 0.0 copy-start.3
  71.3 0.0 all-gather.3.cloned.1.call-update
  71.3 0.6 copy-done.2
  71.9 0.7 fusion.28
  82.8 0.7 fusion.24
  83.6 0.1 compare_reduce_fusion
  83.7 0.0 copy-done.3
  83.7 0.0 copy-done
  83.7 0.3 fusion.21
  83.9 0.7 fusion.27
  84.6 2.6 %all-gather.3.cloned.1.call-done = bf16[24,128,1024]{2,1,0:T(8,128)(2,1)} async-done(((bf16[12,128,1024]{2,1,0:T(8,128)(2,1)}), bf16[24,128,1024]{2,1,0:T(8,128)(2,1)}) %all-gather.3.cloned.1.call-update) | async-done | bytes 6291472 | tf_op jit(solution)/shard_map/all_gather | solution.py:40
  87.2 19.0 %fusion.1 = bf16[1,1,4,128,1024]{4,3,2,1,0:T(8,128)(2,1)} fusion(bf16[2,12,128,1024]{3,2,1,0:T(8,128)(2,1)} %bitcast.64, s32[]{:T(128)S(6)} %add.344, s32[]{:T(128)S(6)} %select_n.52, s32[]{:T(128)S(6)} %select_n.51, s32[]{:T(128)S(6)} %select_n.50, s32[]{:T(128)S(6)} %select_n.49, s32[]{:T(128)S(6)} %select_n.48, s32[]{:T(128)S(6)} %select_n.47, ...), kind=kLoop, calls=%fused_computation.3 | loop fusion | flops 25690112 | bytes 17829988 | tf_op jit(solution)/shard_map/convert_element_type | solution.py:57
  (4 shorter events, 0.0 us)
Async XLA Ops:
  6.5 77.2 %copy-start = (f32[4,8]{1,0:T(4,128)S(1)}, f32[4,8]{1,0:T(4,128)}, u32[]{:S(2)}) copy-start(f32[4,8]{1,0:T(4,128)} %param.10) | copy-start | bytes 388
  6.5 1.6 %copy-start.1 = (bf16[1,1,1,512,1024]{4,3,2,1,0:T(8,128)(2,1)S(1)}, bf16[1,1,1,512,1024]{4,3,2,1,0:T(8,128)(2,1)}, u32[]{:S(2)}) copy-start(bf16[1,1,1,512,1024]{4,3,2,1,0:T(8,128)(2,1)} %param.6) | copy-start | bytes 3145732
  6.5 80.7 %all-gather.3.cloned.1.call-start = ((), (), s32[]{:S(2)}) async-start(), calls=%async_computation.1 | async-start | bytes 9437184 | tf_op jit(solution)/shard_map/all_gather | solution.py:40
  40.9 24.4 %collective-permute-start = (bf16[4,128,1024]{2,1,0:T(8,128)(2,1)S(1)}, bf16[4,128,1024]{2,1,0:T(8,128)(2,1)S(1)}, u32[]{:S(2)}, u32[]{:S(2)}) collective-permute-start(bf16[4,128,1024]{2,1,0:T(8,128)(2,1)S(1)} %bitcast.67), channel_id=1, source_target_pairs={{0,1},{1,2},{2,3},{4,5},{5,6},{6,7},{8,9},{9,10},{10,11},{12,13},{... | collective-permute-start | bytes 3145736 | tf_op jit(solution)/shard_map/ppermute | solution.py:17
  44.4 25.0 %collective-permute-start.1 = (bf16[4,128,1024]{2,1,0:T(8,128)(2,1)S(1)}, bf16[4,128,1024]{2,1,0:T(8,128)(2,1)S(1)}, u32[]{:S(2)}, u32[]{:S(2)}) collective-permute-start(bf16[4,128,1024]{2,1,0:T(8,128)(2,1)S(1)} %bitcast.68), channel_id=1, source_target_pairs={{1,0},{2,1},{3,2},{5,4},{6,5},{7,6},{9,8},{10,9},{11,10},{13,12},{... | collective-permute-start | bytes 3145736 | tf_op jit(solution)/shard_map/ppermute | solution.py:18
  71.3 0.7 copy-start.2
  71.3 12.4 %copy-start.3 = (s32[4]{0:T(128)S(1)}, s32[4]{0:T(128)}, u32[]{:S(2)}) copy-start(s32[4]{0:T(128)} %param.8) | copy-start | bytes 52
Sparse Core Ops, SparseCore 0:
  71.4 15.7 all-gather.2
where the time goes:
time: 114 us; the launch traced here: 113 us
  other arithmetic  29.9 us (26%)
  waiting for transfers between devices  26.1 us (23%)
  between operations  23.8 us (21%)
  blocking collectives  19.1 us (17%)
  local copies, waits for them, and re-layouts  7.35 us (6%)
  starting transfers between devices  5.01 us (4%)
  matrix products  1.74 us (2%)
    ppermute x1, waiting for transfers between devices, with_halo(): before = lax.ppermute(last, axis, up)  19.4 us
    all_to_all x1, blocking collectives, on_device(): lax.all_to_all(payload, 'tile', split_axis=1, concat_axis=0, tiled=True)  19.1 us
    convert_element_type x1, other arithmetic, on_device(): result = (total * colmask[None, None, :]).astype(jnp.bfloat16)  19 us
    unnamed x1, other arithmetic  7.31 us
    ppermute x1, waiting for transfers between devices, with_halo(): after = lax.ppermute(initial, axis, down)  4.18 us
    ppermute x1, starting transfers between devices, with_halo(): before = lax.ppermute(last, axis, up)  3.54 us
    unnamed x12, local copies, waits for them, and re-layouts  3.28 us
    all_gather x1, waiting for transfers between devices, on_device(): extended = lax.all_gather(rimmed[None], 'mom', axis=0, tiled=True)  2.56 us
  transfers between devices with their start and end apart: 3, of which 3 were waited for; matrix products, arithmetic and copies ran while one was open for 2% of the time, Pallas kernels for 0%

commit v1 on v0

--- a/solution.py
+++ b/solution.py
@@ -1,10 +1,275 @@
 import jax
 import jax.numpy as jnp
 from jax import lax
+from jax.experimental import pallas as pl
+from jax.experimental.pallas import tpu as pltpu
 from jax.sharding import PartitionSpec as P
 
 HW = 4
 NW = 8
+PACK = 16
+MESH = pl.DeviceIdType.MESH
+
+
+def fused_kernel(
+    nt, nm, nz, g_ref, gam_ref, shift_ref, off_ref, coup_ref, out_ref,
+    stage, held, fin, tab, a_send, a_recv, z_send, z_recv, f_send, f_recv, own_sem,
+):
+    t, m, z = lax.axis_index("tile"), lax.axis_index("mom"), lax.axis_index("ewin")
+    groups, steps, rb, width = g_ref.shape
+    orb = width // 2
+    has_up, has_down = z < nz - 1, z > 0
+
+    def dev(tt, mm, zz):
+        return {"tile": tt, "mom": mm, "ewin": zz}
+
+    def tile_at(i):
+        return lax.rem(t + i, nt)
+
+    def mom_at(j):
+        return lax.rem(m + j, nm)
+
+    pairs = [(i, j) for i in range(nt) for j in range(nm)]
+    barrier = pltpu.get_barrier_semaphore()
+    for i, j in pairs[1:]:
+        pl.semaphore_signal(barrier, inc=1, device_id=dev(tile_at(i), mom_at(j), z), device_id_type=MESH)
+
+    @pl.when(has_up)
+    def _():
+        pl.semaphore_signal(barrier, inc=1, device_id=dev(t, m, z + 1), device_id_type=MESH)
+
+    @pl.when(has_down)
+    def _():
+        pl.semaphore_signal(barrier, inc=1, device_id=dev(t, m, z - 1), device_id_type=MESH)
+
+    def lesser(r):
+        rows = g_ref[:, r].reshape(groups * rb, width)
+        re = rows[:, :orb].astype(jnp.float32) * gam_ref[...]
+        im = rows[:, orb:].astype(jnp.float32) * gam_ref[...]
+        left_re = jnp.concatenate([re, im], axis=1).astype(jnp.bfloat16)
+        left_im = jnp.concatenate([im, -re], axis=1).astype(jnp.bfloat16)
+        left = jnp.concatenate([left_re, left_im], axis=0)
+        right = g_ref[...].reshape(orb, width)
+        both = lax.dot_general(left, right, (((1,), (1,)), ((), ())), preferred_element_type=jnp.float32)
+        both = both.astype(jnp.bfloat16)
+        half = groups * rb
+        stage[r, :, :, :orb] = both[:half].reshape(groups, rb, orb)
+        stage[r, :, :, orb:] = both[half:].reshape(groups, rb, orb)
+
+    def source(i):
+        return lax.rem(t + nt - i, nt)
+
+    def a_copy(r, i, j):
+        return pltpu.make_async_remote_copy(
+            src_ref=stage.at[r, tile_at(i) * nm + mom_at(j)],
+            dst_ref=held.at[1, t, j, r],
+            send_sem=a_send.at[r, i, j],
+            recv_sem=a_recv.at[r, i, j],
+            device_id=dev(tile_at(i), mom_at(j), z),
+            device_id_type=MESH,
+        )
+
+    def a_landed(r, i, j):
+        p = source(i)
+        return pltpu.make_async_remote_copy(
+            src_ref=stage.at[r, 0],
+            dst_ref=held.at[1, p, j, r],
+            send_sem=a_send.at[r, i, j],
+            recv_sem=a_recv.at[r, i, j],
+            device_id=dev(tile_at(i), mom_at(j), z),
+            device_id_type=MESH,
+        )
+
+    def own_copy(r):
+        return pltpu.make_async_copy(stage.at[r, t * nm + m], held.at[1, t, 0, r], own_sem.at[r])
+
+    def z_copy(r, i, j, up):
+        p = source(i)
+        return pltpu.make_async_remote_copy(
+            src_ref=held.at[1, p, j, r],
+            dst_ref=held.at[0 if up else 2, p, j, r],
+            send_sem=z_send.at[0 if up else 1, r, i, j],
+            recv_sem=z_recv.at[0 if up else 1, r, i, j],
+            device_id=dev(t, m, z + 1 if up else z - 1),
+            device_id_type=MESH,
+        )
+
+    def start_first(r):
+        own_copy(r).start()
+        for i, j in pairs[1:]:
+            a_copy(r, i, j).start()
+
+    lesser(0)
+    pl.semaphore_wait(barrier, nt * nm - 1 + has_up.astype(jnp.int32) + has_down.astype(jnp.int32))
+    start_first(0)
+
+    @pl.loop(1, steps)
+    def _(r):
+        lesser(r)
+        start_first(r)
+
+    @pl.when(jnp.logical_not(has_down))
+    def _():
+        held[0] = jnp.zeros(held.shape[1:], held.dtype)
+
+    @pl.when(jnp.logical_not(has_up))
+    def _():
+        held[2] = jnp.zeros(held.shape[1:], held.dtype)
+
+    def forward(r):
+        for i, j in pairs:
+            if (i, j) == (0, 0):
+                own_copy(r).wait()
+            else:
+                a_landed(r, i, j).wait_recv()
+
+            @pl.when(has_up)
+            def _():
+                z_copy(r, i, j, True).start()
+
+            @pl.when(has_down)
+            def _():
+                z_copy(r, i, j, False).start()
+
+    forward(0)
+    if steps > 1:
+        forward(1)
+
+    shifts = [lax.rem(lax.rem(shift_ref[s], nm) + nm, nm) for s in range(shift_ref.shape[0])]
+    for diff in range(nm):
+        per_off = []
+        for o in range(NW):
+            acc = jnp.float32(0.0)
+            for s in range(len(shifts)):
+                acc = acc + jnp.where(shifts[s] == diff, coup_ref[s, o], 0.0)
+            per_off.append(acc)
+        for d in range(2 * HW + 1):
+            acc = jnp.float32(0.0)
+            for o in range(NW):
+                acc = acc + jnp.where(off_ref[o] + HW == d, per_off[o], 0.0)
+            tab[diff, d] = acc
+
+    def fin_copy(r, kk):
+        return pltpu.make_async_remote_copy(
+            src_ref=fin.at[kk - 1, r],
+            dst_ref=out_ref.at[:, m, r],
+            send_sem=f_send.at[kk - 1, r],
+            recv_sem=f_recv.at[kk - 1, r],
+            device_id=dev(t, mom_at(kk), z),
+            device_id_type=MESH,
+        )
+
+    def fin_landed(r, kk):
+        return pltpu.make_async_remote_copy(
+            src_ref=fin.at[kk - 1, r],
+            dst_ref=out_ref.at[:, lax.rem(m + nm - kk, nm), r],
+            send_sem=f_send.at[kk - 1, r],
+            recv_sem=f_recv.at[kk - 1, r],
+            device_id=dev(t, mom_at(kk), z),
+            device_id_type=MESH,
+        )
+
+    def mix(r):
+        for i, j in pairs:
+            @pl.when(has_down)
+            def _():
+                z_copy(r, i, j, True).wait_recv()
+
+            @pl.when(has_up)
+            def _():
+                z_copy(r, i, j, False).wait_recv()
+
+        weight = [[tab[diff, d] for d in range(2 * HW + 1)] for diff in range(nm)]
+
+        @pl.loop(0, width // 128)
+        def _(c):
+            cols = pl.ds(pl.multiple_of(c * 128, 128), 128)
+            acc = [[None] * nt for _ in range(nm)]
+            for zs in range(3):
+                for p in range(nt):
+                    src = zs * nt + p
+                    for j in range(nm):
+                        x = held[zs, p, j, r, :, cols].astype(jnp.float32)
+                        for kk in range(nm):
+                            for e in range(nt):
+                                if 0 <= src - e <= 2 * HW:
+                                    term = weight[(kk + j) % nm][src - e] * x
+                                    acc[kk][e] = term if acc[kk][e] is None else acc[kk][e] + term
+            for e in range(nt):
+                out_ref[e, m, r, :, cols] = acc[0][e].astype(jnp.bfloat16)
+                for kk in range(1, nm):
+                    fin[kk - 1, r, e, :, cols] = acc[kk][e].astype(jnp.bfloat16)
+
+        for kk in range(1, nm):
+            fin_copy(r, kk).start()
+
+    @pl.loop(0, steps)
+    def _(r):
+        mix(r)
+
+        @pl.when(r + 2 < steps)
+        def _():
+            forward(r + 2)
+
+    @pl.loop(0, steps)
+    def _(r):
+        for kk in range(1, nm):
+            fin_copy(r, kk).wait_send()
+            fin_landed(r, kk).wait_recv()
+        for i, j in pairs:
+            if (i, j) != (0, 0):
+                a_copy(r, i, j).wait_send()
+
+            @pl.when(has_up)
+            def _():
+                z_copy(r, i, j, True).wait_send()
+
+            @pl.when(has_down)
+            def _():
+                z_copy(r, i, j, False).wait_send()
+
+
+def column_mask(tile_nbr, orbitals, per_tile):
+    tile_here = lax.axis_index("tile")
+    neighbours = lax.dynamic_index_in_dim(tile_nbr, tile_here, 0, keepdims=False)
+    coltile = jnp.arange(orbitals, dtype=jnp.int32) // per_tile
+    colmask = jnp.any(coltile[:, None] == neighbours[None, :], axis=1)
+    return jnp.concatenate([colmask, colmask])
+
+
+def fused(green_ret, injection, mom_shift, phon_off, coupling, tile_nbr):
+    nt, nm, nz = lax.axis_size("tile"), lax.axis_size("mom"), lax.axis_size("ewin")
+    orbitals, width = green_ret.shape[3:]
+    per_tile = orbitals // nt
+    steps = per_tile // nm // PACK
+    green = green_ret.reshape(nt * nm, steps, PACK, width)
+    gamma = injection.reshape(1, orbitals)
+    vmem, smem = pl.BlockSpec(memory_space=pltpu.VMEM), pl.BlockSpec(memory_space=pltpu.SMEM)
+    dma = pltpu.SemaphoreType.DMA
+    total = pl.pallas_call(
+        lambda *refs: fused_kernel(nt, nm, nz, *refs),
+        out_shape=jax.ShapeDtypeStruct((nt, nm, steps, PACK, width), jnp.bfloat16),
+        in_specs=[vmem, vmem, smem, smem, smem],
+        out_specs=vmem,
+        scratch_shapes=[
+            pltpu.VMEM((steps, nt * nm, PACK, width), jnp.bfloat16),
+            pltpu.VMEM((3, nt, nm, steps, PACK, width), jnp.bfloat16),
+            pltpu.VMEM((max(nm - 1, 1), steps, nt, PACK, width), jnp.bfloat16),
+            pltpu.SMEM((nm, 2 * HW + 1), jnp.float32),
+            dma((steps, nt, nm)),
+            dma((steps, nt, nm)),
+            dma((2, steps, nt, nm)),
+            dma((2, steps, nt, nm)),
+            dma((max(nm - 1, 1), steps)),
+            dma((max(nm - 1, 1), steps)),
+            dma((steps,)),
+        ],
+        compiler_params=pltpu.CompilerParams(collective_id=0, has_side_effects=True),
+    )(green, gamma, mom_shift, phon_off, coupling)
+    total = total.reshape(nt, per_tile, width)
+    colmask = column_mask(tile_nbr, orbitals, per_tile)
+    result = jnp.where(colmask[None, None, :], total, jnp.zeros((), jnp.bfloat16))
+    return result[None, None]
 
 
 def with_halo(shard, sides, width):
@@ -58,6 +323,19 @@
     return result[None, None]
 
 
+def body_for(mesh):
+    nt, nm = mesh.shape["tile"], mesh.shape["mom"]
+
+    def body(green_ret, *rest):
+        points, orbitals = green_ret.shape[2:4]
+        aligned = orbitals % (nt * nm * PACK) == 0 and orbitals % 128 == 0
+        if aligned and points == 1 and nt == HW:
+            return fused(green_ret, *rest)
+        return on_device(green_ret, *rest)
+
+    return body
+
+
 def solution(mesh):
     placed = (
         P("mom", "ewin", "tile", None, None),
@@ -68,7 +346,7 @@
         P(),
     )
     return jax.shard_map(
-        on_device,
+        body_for(mesh),
         mesh=mesh,
         in_specs=placed,
         out_specs=P("mom", "ewin", None, "tile", None),

time: 114 us -> 40.8 us (0.36)
  Pallas kernels: 0 us -> 37.6 us
  other arithmetic: 29.9 us -> 2.37 us
  waiting for transfers between devices: 26.1 us -> 0 us
  between operations: 23.8 us -> 0.01 us
  blocking collectives: 19.1 us -> 0 us
  local copies, waits for them, and re-layouts: 7.35 us -> 0.69 us
  starting transfers between devices: 5.01 us -> 0 us
  matrix products: 1.74 us -> 0 us
    pallas_call x0 -> x1, Pallas kernels: none -> 37.6 us  [fused(): pl.pallas_call(lambda *refs: fused_kernel(nt, nm, nz, *refs), out_shape=j...]
    ppermute x2 -> x0, waiting for transfers between devices: 23.5 us -> none  [the longest x1 19.4 us: with_halo(): before = lax.ppermute(last, axis, up)]
    all_to_all x1 -> x0, blocking collectives: 19.1 us -> none  [on_device(): lax.all_to_all(payload, 'tile', split_axis=1, concat_axis=0, tiled=True)]
    convert_element_type x1 -> x0, other arithmetic: 19 us -> none  [on_device(): result = (total * colmask[None, None, :]).astype(jnp.bfloat16)]
    unnamed x1 -> x0, other arithmetic: 7.31 us -> none
    ppermute x2 -> x0, starting transfers between devices: 5.01 us -> none  [the longest x1 3.54 us: with_halo(): before = lax.ppermute(last, axis, up)]
    concatenate x4 -> x1, other arithmetic: 3.55 us -> 0.01 us  [column_mask(): return jnp.concatenate([colmask, colmask])]
    unnamed x12 -> x2, local copies, waits for them, and re-layouts: 3.28 us -> 0.68 us
  transfers between devices with their start and end apart: 3 -> 0, of which waited for: 3 -> 0; matrix products, arithmetic and copies ran while one was open for 2% -> 0% of each run, Pallas kernels for 0% -> 0%
where the time goes in v1:
time: 40.8 us; the launch traced here: 40.6 us
  Pallas kernels  37.6 us (92%)
  other arithmetic  2.37 us (6%)
  local copies, waits for them, and re-layouts  0.69 us (2%)
    pallas_call x1, Pallas kernels, fused(): pl.pallas_call(lambda *refs: fused_kernel(nt, nm, nz, *refs), out_shape=j...  37.6 us
    select_n x1, other arithmetic, fused(): jnp.where(colmask[None, None, :], total, jnp.zeros((), jnp.bfloat16))  2.27 us

profile of v1, /device:TPU:0, one launch (start us, length us, event | category | flops | bytes accessed | tf_op | source)
XLA Modules:
  0.0 40.6 jit_solution(11847219023930894899)
XLA Ops:
  0.0 0.0 copy-start
  0.0 0.7 %copy-done = s32[4,4]{1,0:T(4,128)S(1)} copy-done((s32[4,4]{1,0:T(4,128)S(1)}, s32[4,4]{1,0:T(4,128)}, u32[]{:S(2)}) %copy-start) | copy-done | bytes 88
  0.7 0.1 compare_reduce_fusion
  0.8 37.6 %shard_map.64 = bf16[4,2,4,16,1024]{4,3,2,1,0:T(8,128)(2,1)} custom-call(bf16[8,4,16,1024]{3,2,1,0:T(8,128)(2,1)} %bitcast.6, f32[1,512]{1,0:T(1,128)} %bitcast.7, s32[4]{0:T(128)} %refs_2_.1, s32[8]{0:T(128)} %refs_3_.1, f32[4,8]{1,0:T(4,128)} %refs_4_.1), custom_call_target="tpu_custom_call" | custom-call | tf_op jit(solution)/shard_map/pallas_call | solution.py:249
  38.4 2.3 %broadcast_select_fusion = bf16[1,1,4,128,1024]{4,3,2,1,0:T(8,128)(2,1)} fusion(bf16[1,1,4,128,1024]{4,3,2,1,0:T(8,128)(2,1)} %bitcast.5, pred[1024]{0:T(1024)(128)(4,1)S(1)} %pad_add_fusion), kind=kLoop, calls=%fused_computation | loop fusion | flops 524288 | bytes 2098176 | tf_op jit(solution)/shard_map/jit(_where)/select_n | solution.py:271
  (3 shorter events, 0.0 us)
Async XLA Ops:
  0.0 0.7 %copy-start = (s32[4,4]{1,0:T(4,128)S(1)}, s32[4,4]{1,0:T(4,128)}, u32[]{:S(2)}) copy-start(s32[4,4]{1,0:T(4,128)} %param.11) | copy-start | bytes 196

commit v2 on v0

--- a/solution.py
+++ b/solution.py
@@ -1,10 +1,357 @@
 import jax
 import jax.numpy as jnp
 from jax import lax
+from jax.experimental import pallas as pl
+from jax.experimental.pallas import tpu as pltpu
 from jax.sharding import PartitionSpec as P
 
 HW = 4
 NW = 8
+LANES = 128
+PACK = 16
+MESH = pl.DeviceIdType.MESH
+
+
+def fused_kernel(
+    nt, nm, nz, g_ref, gam_ref, shift_ref, off_ref, coup_ref, out_ref,
+    left, stage, cross, held, fin, parts, tab,
+    a_send, a_recv, z_send, z_recv, f_send, f_recv, own_sem,
+):
+    t, m, z = lax.axis_index("tile"), lax.axis_index("mom"), lax.axis_index("ewin")
+    orb, width = g_ref.shape
+    tall = orb // nt
+    hr = tall // nm
+    qr = hr // 2
+    rows_of = ((0, hr), (hr, qr), (hr + qr, hr))
+    has_up, has_down = z < nz - 1, z > 0
+
+    def dev(tt, mm, zz):
+        return {"tile": tt, "mom": mm, "ewin": zz}
+
+    def order(q):
+        return q + (q // 2) * (5 - 2 * q)
+
+    ring = order(t)
+
+    def tile_at(i):
+        return order(lax.rem(ring + i, nt))
+
+    def mom_at(j):
+        return lax.rem(m + j, nm)
+
+    pairs = [(i, j) for i in range(nt) for j in range(nm)]
+    barrier = pltpu.get_barrier_semaphore()
+    for i, j in pairs[1:]:
+        pl.semaphore_signal(barrier, inc=1, device_id=dev(tile_at(i), mom_at(j), z), device_id_type=MESH)
+
+    @pl.when(has_up)
+    def _():
+        pl.semaphore_signal(barrier, inc=1, device_id=dev(t, m, z + 1), device_id_type=MESH)
+
+    @pl.when(has_down)
+    def _():
+        pl.semaphore_signal(barrier, inc=1, device_id=dev(t, m, z - 1), device_id_type=MESH)
+
+    def tile_rows(tile):
+        return pl.ds(pl.multiple_of(tile * tall, tall), tall)
+
+    def product(slot, tile):
+        both = lax.dot_general(
+            left[slot], g_ref[tile_rows(tile), :], (((1,), (1,)), ((), ())), preferred_element_type=jnp.float32
+        ).astype(jnp.bfloat16)
+        return both[:tall], both[tall:]
+
+    def compute_first(i):
+        rows = g_ref[tile_rows(tile_at(i)), :]
+        re = rows[:, :orb].astype(jnp.float32) * gam_ref[...]
+        im = rows[:, orb:].astype(jnp.float32) * gam_ref[...]
+        left[i, :tall, :orb] = re.astype(jnp.bfloat16)
+        left[i, :tall, orb:] = im.astype(jnp.bfloat16)
+        left[i, tall:, :orb] = im.astype(jnp.bfloat16)
+        left[i, tall:, orb:] = (-re).astype(jnp.bfloat16)
+        put(0, i, tile_at(i + 1))
+
+    def put(which, i, tile):
+        re, im = product(i, tile)
+        stage[which, i, :, :, :tall] = re.reshape(nm, hr, tall)
+        stage[which, i, :, :, tall:] = im.reshape(nm, hr, tall)
+
+    def compute_cross(a):
+        re, im = product(lax.rem(a - ring + nt, nt), order(a + 2))
+        cross[a, :, :, :tall] = re.reshape(2 * nm, qr, tall)
+        cross[a, :, :, tall:] = im.reshape(2 * nm, qr, tall)
+
+    def unit_source(u, i, j):
+        c = mom_at(j)
+        if u == 1:
+            q = lax.rem(ring + i, nt)
+            return cross.at[lax.rem(q, 2), (q // 2) * nm + c]
+        return stage.at[u // 2, i, c]
+
+    def a_copy(u, i, j, p):
+        lo, n = rows_of[u]
+        return pltpu.make_async_remote_copy(
+            src_ref=unit_source(u, i, j),
+            dst_ref=held.at[1, p, j, pl.ds(lo, n)],
+            send_sem=a_send.at[u, i, j],
+            recv_sem=a_recv.at[u, i, j],
+            device_id=dev(tile_at(i), mom_at(j), z),
+            device_id_type=MESH,
+        )
+
+    def own_copy(u):
+        lo, n = rows_of[u]
+        return pltpu.make_async_copy(unit_source(u, 0, 0), held.at[1, t, 0, pl.ds(lo, n)], own_sem.at[u])
+
+    def z_copy(u, i, j, up):
+        p = tile_at(nt - i)
+        lo, n = rows_of[u]
+        return pltpu.make_async_remote_copy(
+            src_ref=held.at[1, p, j, pl.ds(lo, n)],
+            dst_ref=held.at[0 if up else 2, p, j, pl.ds(lo, n)],
+            send_sem=z_send.at[0 if up else 1, u, i, j],
+            recv_sem=z_recv.at[0 if up else 1, u, i, j],
+            device_id=dev(t, m, z + 1 if up else z - 1),
+            device_id_type=MESH,
+        )
+
+    def send_slot(u, i):
+        for j in range(nm):
+            if (i, j) == (0, 0):
+                own_copy(u).start()
+            else:
+                a_copy(u, i, j, t).start()
+
+    def forward(u):
+        for i, j in pairs:
+            if (i, j) == (0, 0):
+                own_copy(u).wait()
+            else:
+                a_copy(u, i, j, tile_at(nt - i)).wait_recv()
+
+            @pl.when(has_up)
+            def _():
+                z_copy(u, i, j, True).start()
+
+            @pl.when(has_down)
+            def _():
+                z_copy(u, i, j, False).start()
+
+    for i in range(nt):
+        compute_first(i)
+        if i == 0:
+            pl.semaphore_wait(barrier, nt * nm - 1 + has_up.astype(jnp.int32) + has_down.astype(jnp.int32))
+        send_slot(0, i)
+    for a in range(2):
+        compute_cross(a)
+    for i in range(nt):
+        send_slot(1, i)
+    forward(0)
+    for i in range(nt):
+        put(1, i, tile_at(i))
+        send_slot(2, i)
+    forward(1)
+
+    @pl.when(jnp.logical_not(has_down))
+    def _():
+        held[0] = jnp.zeros(held.shape[1:], held.dtype)
+
+    @pl.when(jnp.logical_not(has_up))
+    def _():
+        held[2] = jnp.zeros(held.shape[1:], held.dtype)
+
+    shifts = [lax.rem(lax.rem(shift_ref[s], nm) + nm, nm) for s in range(shift_ref.shape[0])]
+    for diff in range(nm):
+        per_off = []
+        for o in range(NW):
+            acc = jnp.float32(0.0)
+            for s in range(len(shifts)):
+                acc = acc + jnp.where(shifts[s] == diff, coup_ref[s, o], 0.0)
+            per_off.append(acc)
+        for d in range(2 * HW + 1):
+            acc = jnp.float32(0.0)
+            for o in range(NW):
+                acc = acc + jnp.where(off_ref[o] + HW == d, per_off[o], 0.0)
+            tab[diff, d] = acc
+
+    def part_lo(u, who):
+        if u == 1:
+            return pl.multiple_of(((ring // 2) * nm + who) * qr, qr)
+        return pl.multiple_of(who * hr, hr)
+
+    def near_copy(u, kk, who):
+        lo, n = rows_of[u]
+        return pltpu.make_async_remote_copy(
+            src_ref=fin.at[kk, :, pl.ds(lo, n)],
+            dst_ref=parts.at[u, :, pl.ds(part_lo(u, who), n)],
+            send_sem=f_send.at[0, u, kk],
+            recv_sem=f_recv.at[0, u, kk],
+            device_id=dev(t, mom_at(kk), z),
+            device_id_type=MESH,
+        )
+
+    def far_copy(u, kk, lo_there):
+        lo, n = rows_of[u]
+        return pltpu.make_async_remote_copy(
+            src_ref=fin.at[kk, :, pl.ds(lo, n)],
+            dst_ref=parts.at[1 if u == 1 else 3, :, pl.ds(lo_there, n)],
+            send_sem=f_send.at[1, u, kk],
+            recv_sem=f_recv.at[1, u, kk],
+            device_id=dev(tile_at(1 + u), mom_at(kk), z),
+            device_id_type=MESH,
+        )
+
+    def far_lo(u, who):
+        if u == 1:
+            return pl.multiple_of(((1 - ring // 2) * nm + who) * qr, qr)
+        return pl.multiple_of(who * hr, hr)
+
+    def mix(u):
+        for i, j in pairs:
+            @pl.when(has_down)
+            def _():
+                z_copy(u, i, j, True).wait_recv()
+
+            @pl.when(has_up)
+            def _():
+                z_copy(u, i, j, False).wait_recv()
+
+        lo, n = rows_of[u]
+        base = part_lo(u, m)
+        weight = [[tab[diff, d] for d in range(2 * HW + 1)] for diff in range(nm)]
+        wide = 2 * tall // LANES
+
+        @pl.loop(0, n // PACK * wide)
+        def _(step):
+            r = pl.multiple_of((step // wide) * PACK, PACK)
+            rows = pl.ds(pl.multiple_of(lo + r, PACK), PACK)
+            cols = pl.ds(pl.multiple_of((step % wide) * LANES, LANES), LANES)
+            acc = [[None] * nt for _ in range(nm)]
+            for zs in range(3):
+                for p in range(nt):
+                    src = zs * nt + p
+                    for j in range(nm):
+                        x = held[zs, p, j, rows, cols].astype(jnp.float32)
+                        for kk in range(nm):
+                            for e in range(nt):
+                                if 0 <= src - e <= 2 * HW:
+                                    term = weight[(kk + j) % nm][src - e] * x
+                                    acc[kk][e] = term if acc[kk][e] is None else acc[kk][e] + term
+            for e in range(nt):
+                for kk in range(nm):
+                    value = acc[kk][e].astype(jnp.bfloat16)
+                    if kk == 0:
+                        parts[u, e, pl.ds(pl.multiple_of(base + r, PACK), PACK), cols] = value
+                    if kk > 0 or u < 2:
+                        fin[kk, e, rows, cols] = value
+
+        for kk in range(nm):
+            if u < 2:
+                far_copy(u, kk, part_lo(u, m)).start()
+            if kk > 0:
+                near_copy(u, kk, m).start()
+
+    def landed(u):
+        for kk in range(nm):
+            who = lax.rem(m + nm - kk, nm)
+            if u < 2:
+                far_copy(u, kk, far_lo(u, who)).wait_recv()
+            if kk > 0:
+                near_copy(u, kk, who).wait_recv()
+
+    def store(part, tile, flip):
+        @pl.loop(0, nt)
+        def _(e):
+            re, im = parts[part, e, :, :tall], parts[part, e, :, tall:]
+            if flip:
+                re = re.astype(jnp.float32).T.astype(jnp.bfloat16)
+                im = (-(im.astype(jnp.float32).T)).astype(jnp.bfloat16)
+            out_ref[e, :, pl.ds(pl.multiple_of(tile * tall, tall), tall)] = re
+            out_ref[e, :, pl.ds(pl.multiple_of(orb + tile * tall, tall), tall)] = im
+
+    mix(0)
+    forward(2)
+    mix(1)
+    landed(0)
+    store(0, tile_at(1), False)
+    store(3, tile_at(nt - 1), True)
+    landed(1)
+
+    @pl.when(ring < 2)
+    def _():
+        store(1, tile_at(2), False)
+
+    @pl.when(ring >= 2)
+    def _():
+        store(1, tile_at(2), True)
+
+    mix(2)
+    landed(2)
+    store(2, t, False)
+
+    for u in range(3):
+        for kk in range(nm):
+            if u < 2:
+                far_copy(u, kk, part_lo(u, m)).wait_send()
+            if kk > 0:
+                near_copy(u, kk, m).wait_send()
+        for i, j in pairs:
+            if (i, j) != (0, 0):
+                a_copy(u, i, j, t).wait_send()
+
+            @pl.when(has_up)
+            def _():
+                z_copy(u, i, j, True).wait_send()
+
+            @pl.when(has_down)
+            def _():
+                z_copy(u, i, j, False).wait_send()
+
+
+def column_mask(tile_nbr, orbitals, per_tile):
+    tile_here = lax.axis_index("tile")
+    neighbours = lax.dynamic_index_in_dim(tile_nbr, tile_here, 0, keepdims=False)
+    coltile = jnp.arange(orbitals, dtype=jnp.int32) // per_tile
+    colmask = jnp.any(coltile[:, None] == neighbours[None, :], axis=1)
+    return jnp.concatenate([colmask, colmask])
+
+
+def fused(green_ret, injection, mom_shift, phon_off, coupling, tile_nbr):
+    nt, nm, nz = lax.axis_size("tile"), lax.axis_size("mom"), lax.axis_size("ewin")
+    orbitals, width = green_ret.shape[3:]
+    tall = orbitals // nt
+    hr = tall // nm
+    qr = hr // 2
+    green = green_ret.reshape(orbitals, width)
+    gamma = injection.reshape(1, orbitals)
+    vmem, smem = pl.BlockSpec(memory_space=pltpu.VMEM), pl.BlockSpec(memory_space=pltpu.SMEM)
+    dma = pltpu.SemaphoreType.DMA
+    total = pl.pallas_call(
+        lambda *refs: fused_kernel(nt, nm, nz, *refs),
+        out_shape=jax.ShapeDtypeStruct((nt, tall, width), jnp.bfloat16),
+        in_specs=[vmem, vmem, smem, smem, smem],
+        out_specs=vmem,
+        scratch_shapes=[
+            pltpu.VMEM((nt, 2 * tall, width), jnp.bfloat16),
+            pltpu.VMEM((2, nt, nm, hr, 2 * tall), jnp.bfloat16),
+            pltpu.VMEM((2, 2 * nm, qr, 2 * tall), jnp.bfloat16),
+            pltpu.VMEM((3, nt, nm, 2 * hr + qr, 2 * tall), jnp.bfloat16),
+            pltpu.VMEM((nm, nt, 2 * hr + qr, 2 * tall), jnp.bfloat16),
+            pltpu.VMEM((4, nt, tall, 2 * tall), jnp.bfloat16),
+            pltpu.SMEM((nm, 2 * HW + 1), jnp.float32),
+            dma((3, nt, nm)),
+            dma((3, nt, nm)),
+            dma((2, 3, nt, nm)),
+            dma((2, 3, nt, nm)),
+            dma((2, 3, nm)),
+            dma((2, 3, nm)),
+            dma((3,)),
+        ],
+        compiler_params=pltpu.CompilerParams(collective_id=0, has_side_effects=True),
+    )(green, gamma, mom_shift, phon_off, coupling)
+    colmask = column_mask(tile_nbr, orbitals, tall)
+    result = jnp.where(colmask[None, None, :], total, jnp.zeros((), jnp.bfloat16))
+    return result[None, None]
 
 
 def with_halo(shard, sides, width):
@@ -58,6 +405,19 @@
     return result[None, None]
 
 
+def body_for(mesh):
+    nt, nm = mesh.shape["tile"], mesh.shape["mom"]
+
+    def body(green_ret, *rest):
+        points, orbitals = green_ret.shape[2:4]
+        aligned = orbitals % (nt * LANES) == 0 and orbitals % (nt * nm * 2 * PACK) == 0
+        if aligned and points == 1 and nt == HW:
+            return fused(green_ret, *rest)
+        return on_device(green_ret, *rest)
+
+    return body
+
+
 def solution(mesh):
     placed = (
         P("mom", "ewin", "tile", None, None),
@@ -68,7 +428,7 @@
         P(),
     )
     return jax.shard_map(
-        on_device,
+        body_for(mesh),
         mesh=mesh,
         in_specs=placed,
         out_specs=P("mom", "ewin", None, "tile", None),

time: 114 us -> 35.4 us (0.31)
  Pallas kernels: 0 us -> 32.1 us
  other arithmetic: 29.9 us -> 2.37 us
  waiting for transfers between devices: 26.1 us -> 0 us
  between operations: 23.8 us -> 0.01 us
  blocking collectives: 19.1 us -> 0 us
  local copies, waits for them, and re-layouts: 7.35 us -> 0.69 us
  starting transfers between devices: 5.01 us -> 0 us
  matrix products: 1.74 us -> 0 us
    pallas_call x0 -> x1, Pallas kernels: none -> 32.1 us  [fused(): pl.pallas_call(lambda *refs: fused_kernel(nt, nm, nz, *refs), out_shape=j...]
    ppermute x2 -> x0, waiting for transfers between devices: 23.5 us -> none  [the longest x1 19.4 us: with_halo(): before = lax.ppermute(last, axis, up)]
    all_to_all x1 -> x0, blocking collectives: 19.1 us -> none  [on_device(): lax.all_to_all(payload, 'tile', split_axis=1, concat_axis=0, tiled=True)]
    convert_element_type x1 -> x0, other arithmetic: 19 us -> none  [on_device(): result = (total * colmask[None, None, :]).astype(jnp.bfloat16)]
    unnamed x1 -> x0, other arithmetic: 7.31 us -> none
    ppermute x2 -> x0, starting transfers between devices: 5.01 us -> none  [the longest x1 3.54 us: with_halo(): before = lax.ppermute(last, axis, up)]
    concatenate x4 -> x1, other arithmetic: 3.55 us -> 0.01 us  [column_mask(): return jnp.concatenate([colmask, colmask])]
    unnamed x12 -> x2, local copies, waits for them, and re-layouts: 3.28 us -> 0.68 us
  transfers between devices with their start and end apart: 3 -> 0, of which waited for: 3 -> 0; matrix products, arithmetic and copies ran while one was open for 2% -> 0% of each run, Pallas kernels for 0% -> 0%
where the time goes in v2:
time: 35.4 us; the launch traced here: 35.2 us
  Pallas kernels  32.1 us (91%)
  other arithmetic  2.37 us (7%)
  local copies, waits for them, and re-layouts  0.69 us (2%)
    pallas_call x1, Pallas kernels, fused(): pl.pallas_call(lambda *refs: fused_kernel(nt, nm, nz, *refs), out_shape=j...  32.1 us
    broadcast_in_dim x1, other arithmetic, fused(): return result[None, None]  2.27 us

profile of v2, /device:TPU:0, one launch (start us, length us, event | category | flops | bytes accessed | tf_op | source)
XLA Modules:
  0.0 35.2 jit_solution(3642150705758434623)
XLA Ops:
  0.0 0.0 copy-start
  0.0 0.7 %copy-done = s32[4,4]{1,0:T(4,128)S(1)} copy-done((s32[4,4]{1,0:T(4,128)S(1)}, s32[4,4]{1,0:T(4,128)}, u32[]{:S(2)}) %copy-start) | copy-done | bytes 88
  0.7 0.1 compare_reduce_fusion
  0.8 32.1 %shard_map.64 = bf16[4,128,1024]{2,1,0:T(8,128)(2,1)} custom-call(bf16[512,1024]{1,0:T(8,128)(2,1)} %bitcast.6, f32[1,512]{1,0:T(1,128)} %bitcast.7, s32[4]{0:T(128)} %refs_2_.1, s32[8]{0:T(128)} %refs_3_.1, f32[4,8]{1,0:T(4,128)} %refs_4_.1), custom_call_target="tpu_custom_call" | custom-call | tf_op jit(solution)/shard_map/pallas_call | solution.py:329
  32.9 2.3 %select_bitcast_fusion = bf16[1,1,4,128,1024]{4,3,2,1,0:T(8,128)(2,1)} fusion(bf16[4,128,1024]{2,1,0:T(8,128)(2,1)} %shard_map.64, pred[1024]{0:T(1024)(128)(4,1)S(1)} %pad_add_fusion), kind=kLoop, calls=%fused_computation | loop fusion | flops 524288 | bytes 2098176 | tf_op jit(solution)/shard_map/broadcast_in_dim | solution.py:354
  (3 shorter events, 0.0 us)
Async XLA Ops:
  0.0 0.7 %copy-start = (s32[4,4]{1,0:T(4,128)S(1)}, s32[4,4]{1,0:T(4,128)}, u32[]{:S(2)}) copy-start(s32[4,4]{1,0:T(4,128)} %param.11) | copy-start | bytes 196

commit v3 on v2

--- a/solution.py
+++ b/solution.py
@@ -14,15 +14,13 @@
 
 def fused_kernel(
     nt, nm, nz, g_ref, gam_ref, shift_ref, off_ref, coup_ref, out_ref,
-    left, stage, cross, held, fin, parts, tab,
+    left, stage, cross, diag, held, fin, parts, tab,
     a_send, a_recv, z_send, z_recv, f_send, f_recv, own_sem,
 ):
     t, m, z = lax.axis_index("tile"), lax.axis_index("mom"), lax.axis_index("ewin")
     orb, width = g_ref.shape
     tall = orb // nt
-    hr = tall // nm
-    qr = hr // 2
-    rows_of = ((0, hr), (hr, qr), (hr + qr, hr))
+    qr = tall // nm // 2
     has_up, has_down = z < nz - 1, z > 0
 
     def dev(tt, mm, zz):
@@ -58,7 +56,7 @@
     def product(slot, tile):
         both = lax.dot_general(
             left[slot], g_ref[tile_rows(tile), :], (((1,), (1,)), ((), ())), preferred_element_type=jnp.float32
-        ).astype(jnp.bfloat16)
+        )
         return both[:tall], both[tall:]
 
     def compute_first(i):
@@ -69,27 +67,41 @@
         left[i, :tall, orb:] = im.astype(jnp.bfloat16)
         left[i, tall:, :orb] = im.astype(jnp.bfloat16)
         left[i, tall:, orb:] = (-re).astype(jnp.bfloat16)
-        put(0, i, tile_at(i + 1))
-
-    def put(which, i, tile):
+        put(i, tile_at(i + 1))
+
+    def triangle():
+        return (lax.broadcasted_iota(jnp.int32, (tall, tall), d) for d in (0, 1))
+
+    def put(i, tile):
         re, im = product(i, tile)
-        stage[which, i, :, :, :tall] = re.reshape(nm, hr, tall)
-        stage[which, i, :, :, tall:] = im.reshape(nm, hr, tall)
+        stage[i, :, :, :, :tall] = re.reshape(2, nm, qr, tall).astype(jnp.bfloat16)
+        stage[i, :, :, :, tall:] = im.reshape(2, nm, qr, tall).astype(jnp.bfloat16)
+
+    def put_diagonal(i):
+        re, im = product(i, tile_at(i))
+        row, col = triangle()
+        both = jnp.where(row > col, im, re).reshape(nm, 2, qr, tall).astype(jnp.bfloat16)
+        diag[i, :, :, :tall] = both[:, 0]
+        diag[i, :, :, tall:] = both[:, 1]
 
     def compute_cross(a):
         re, im = product(lax.rem(a - ring + nt, nt), order(a + 2))
-        cross[a, :, :, :tall] = re.reshape(2 * nm, qr, tall)
-        cross[a, :, :, tall:] = im.reshape(2 * nm, qr, tall)
+        cross[a, :, :, :tall] = re.reshape(2 * nm, qr, tall).astype(jnp.bfloat16)
+        cross[a, :, :, tall:] = im.reshape(2 * nm, qr, tall).astype(jnp.bfloat16)
 
     def unit_source(u, i, j):
         c = mom_at(j)
+        if u == 0:
+            return stage.at[i, 0, c]
         if u == 1:
+            return stage.at[(i - 1) % nt, 1, c]
+        if u == 2:
             q = lax.rem(ring + i, nt)
             return cross.at[lax.rem(q, 2), (q // 2) * nm + c]
-        return stage.at[u // 2, i, c]
+        return diag.at[i, c]
 
     def a_copy(u, i, j, p):
-        lo, n = rows_of[u]
+        lo, n = u * qr, qr
         return pltpu.make_async_remote_copy(
             src_ref=unit_source(u, i, j),
             dst_ref=held.at[1, p, j, pl.ds(lo, n)],
@@ -100,12 +112,12 @@
         )
 
     def own_copy(u):
-        lo, n = rows_of[u]
+        lo, n = u * qr, qr
         return pltpu.make_async_copy(unit_source(u, 0, 0), held.at[1, t, 0, pl.ds(lo, n)], own_sem.at[u])
 
     def z_copy(u, i, j, up):
         p = tile_at(nt - i)
-        lo, n = rows_of[u]
+        lo, n = u * qr, qr
         return pltpu.make_async_remote_copy(
             src_ref=held.at[1, p, j, pl.ds(lo, n)],
             dst_ref=held.at[0 if up else 2, p, j, pl.ds(lo, n)],
@@ -142,14 +154,16 @@
         if i == 0:
             pl.semaphore_wait(barrier, nt * nm - 1 + has_up.astype(jnp.int32) + has_down.astype(jnp.int32))
         send_slot(0, i)
+    for i in range(nt):
+        send_slot(1, i)
     for a in range(2):
         compute_cross(a)
     for i in range(nt):
-        send_slot(1, i)
+        send_slot(2, i)
     forward(0)
     for i in range(nt):
-        put(1, i, tile_at(i))
-        send_slot(2, i)
+        put_diagonal(i)
+        send_slot(3, i)
     forward(1)
 
     @pl.when(jnp.logical_not(has_down))
@@ -174,13 +188,12 @@
                 acc = acc + jnp.where(off_ref[o] + HW == d, per_off[o], 0.0)
             tab[diff, d] = acc
 
-    def part_lo(u, who):
-        if u == 1:
-            return pl.multiple_of(((ring // 2) * nm + who) * qr, qr)
-        return pl.multiple_of(who * hr, hr)
+    def part_lo(u, who, mine=True):
+        block = (0, 1, ring // 2 if mine else 1 - ring // 2, 0)[u]
+        return pl.multiple_of((block * nm + who) * qr, qr)
 
     def near_copy(u, kk, who):
-        lo, n = rows_of[u]
+        lo, n = u * qr, qr
         return pltpu.make_async_remote_copy(
             src_ref=fin.at[kk, :, pl.ds(lo, n)],
             dst_ref=parts.at[u, :, pl.ds(part_lo(u, who), n)],
@@ -191,20 +204,15 @@
         )
 
     def far_copy(u, kk, lo_there):
-        lo, n = rows_of[u]
+        lo, n = u * qr, qr
         return pltpu.make_async_remote_copy(
             src_ref=fin.at[kk, :, pl.ds(lo, n)],
-            dst_ref=parts.at[1 if u == 1 else 3, :, pl.ds(lo_there, n)],
+            dst_ref=parts.at[(1, 0, 2)[u], :, pl.ds(lo_there, n)],
             send_sem=f_send.at[1, u, kk],
             recv_sem=f_recv.at[1, u, kk],
-            device_id=dev(tile_at(1 + u), mom_at(kk), z),
+            device_id=dev(tile_at((1, nt - 1, 2)[u]), mom_at(kk), z),
             device_id_type=MESH,
         )
-
-    def far_lo(u, who):
-        if u == 1:
-            return pl.multiple_of(((1 - ring // 2) * nm + who) * qr, qr)
-        return pl.multiple_of(who * hr, hr)
 
     def mix(u):
         for i, j in pairs:
@@ -216,7 +224,7 @@
             def _():
                 z_copy(u, i, j, False).wait_recv()
 
-        lo, n = rows_of[u]
+        lo, n = u * qr, qr
         base = part_lo(u, m)
         weight = [[tab[diff, d] for d in range(2 * HW + 1)] for diff in range(nm)]
         wide = 2 * tall // LANES
@@ -242,11 +250,11 @@
                     value = acc[kk][e].astype(jnp.bfloat16)
                     if kk == 0:
                         parts[u, e, pl.ds(pl.multiple_of(base + r, PACK), PACK), cols] = value
-                    if kk > 0 or u < 2:
+                    if kk > 0 or u < 3:
                         fin[kk, e, rows, cols] = value
 
         for kk in range(nm):
-            if u < 2:
+            if u < 3:
                 far_copy(u, kk, part_lo(u, m)).start()
             if kk > 0:
                 near_copy(u, kk, m).start()
@@ -254,8 +262,8 @@
     def landed(u):
         for kk in range(nm):
             who = lax.rem(m + nm - kk, nm)
-            if u < 2:
-                far_copy(u, kk, far_lo(u, who)).wait_recv()
+            if u < 3:
+                far_copy(u, kk, part_lo(u, who, False)).wait_recv()
             if kk > 0:
                 near_copy(u, kk, who).wait_recv()
 
@@ -269,29 +277,47 @@
             out_ref[e, :, pl.ds(pl.multiple_of(tile * tall, tall), tall)] = re
             out_ref[e, :, pl.ds(pl.multiple_of(orb + tile * tall, tall), tall)] = im
 
+    def store_diagonal():
+        row, col = triangle()
+
+        @pl.loop(0, nt)
+        def _(e):
+            packed = [
+                parts[3, e, c * qr : (c + 1) * qr, h * tall : (h + 1) * tall] for c in range(nm) for h in range(2)
+            ]
+            both = jnp.concatenate(packed, axis=0).astype(jnp.float32)
+            turned = both.T
+            re = jnp.where(row > col, turned, both)
+            im = jnp.where(row > col, both, jnp.where(row < col, -turned, 0.0))
+            out_ref[e, :, pl.ds(pl.multiple_of(t * tall, tall), tall)] = re.astype(jnp.bfloat16)
+            out_ref[e, :, pl.ds(pl.multiple_of(orb + t * tall, tall), tall)] = im.astype(jnp.bfloat16)
+
+    forward(2)
     mix(0)
-    forward(2)
+    forward(3)
     mix(1)
+    mix(2)
     landed(0)
+    landed(1)
     store(0, tile_at(1), False)
-    store(3, tile_at(nt - 1), True)
-    landed(1)
+    store(1, tile_at(nt - 1), True)
+    mix(3)
+    landed(2)
 
     @pl.when(ring < 2)
     def _():
-        store(1, tile_at(2), False)
+        store(2, tile_at(2), False)
 
     @pl.when(ring >= 2)
     def _():
-        store(1, tile_at(2), True)
-
-    mix(2)
-    landed(2)
-    store(2, t, False)
-
-    for u in range(3):
+        store(2, tile_at(2), True)
+
+    landed(3)
+    store_diagonal()
+
+    for u in range(4):
         for kk in range(nm):
-            if u < 2:
+            if u < 3:
                 far_copy(u, kk, part_lo(u, m)).wait_send()
             if kk > 0:
                 near_copy(u, kk, m).wait_send()
@@ -320,8 +346,7 @@
     nt, nm, nz = lax.axis_size("tile"), lax.axis_size("mom"), lax.axis_size("ewin")
     orbitals, width = green_ret.shape[3:]
     tall = orbitals // nt
-    hr = tall // nm
-    qr = hr // 2
+    qr = tall // nm // 2
     green = green_ret.reshape(orbitals, width)
     gamma = injection.reshape(1, orbitals)
     vmem, smem = pl.BlockSpec(memory_space=pltpu.VMEM), pl.BlockSpec(memory_space=pltpu.SMEM)
@@ -333,19 +358,20 @@
         out_specs=vmem,
         scratch_shapes=[
             pltpu.VMEM((nt, 2 * tall, width), jnp.bfloat16),
-            pltpu.VMEM((2, nt, nm, hr, 2 * tall), jnp.bfloat16),
+            pltpu.VMEM((nt, 2, nm, qr, 2 * tall), jnp.bfloat16),
             pltpu.VMEM((2, 2 * nm, qr, 2 * tall), jnp.bfloat16),
-            pltpu.VMEM((3, nt, nm, 2 * hr + qr, 2 * tall), jnp.bfloat16),
-            pltpu.VMEM((nm, nt, 2 * hr + qr, 2 * tall), jnp.bfloat16),
+            pltpu.VMEM((nt, nm, qr, 2 * tall), jnp.bfloat16),
+            pltpu.VMEM((3, nt, nm, 4 * qr, 2 * tall), jnp.bfloat16),
+            pltpu.VMEM((nm, nt, 4 * qr, 2 * tall), jnp.bfloat16),
             pltpu.VMEM((4, nt, tall, 2 * tall), jnp.bfloat16),
             pltpu.SMEM((nm, 2 * HW + 1), jnp.float32),
-            dma((3, nt, nm)),
-            dma((3, nt, nm)),
-            dma((2, 3, nt, nm)),
-            dma((2, 3, nt, nm)),
-            dma((2, 3, nm)),
-            dma((2, 3, nm)),
-            dma((3,)),
+            dma((4, nt, nm)),
+            dma((4, nt, nm)),
+            dma((2, 4, nt, nm)),
+            dma((2, 4, nt, nm)),
+            dma((2, 4, nm)),
+            dma((2, 4, nm)),
+            dma((4,)),
         ],
         compiler_params=pltpu.CompilerParams(collective_id=0, has_side_effects=True),
     )(green, gamma, mom_shift, phon_off, coupling)

time: 35.4 us -> 31.4 us (0.89)
  Pallas kernels: 32.1 us -> 28 us
    pallas_call x1, Pallas kernels: 32.1 us -> 28 us  [fused(): pl.pallas_call(lambda *refs: fused_kernel(nt, nm, nz, *refs), out_shape=j...]
where the time goes in v3:
time: 31.4 us; the launch traced here: 31.1 us
  Pallas kernels  28 us (89%)
  other arithmetic  2.37 us (8%)
  local copies, waits for them, and re-layouts  0.69 us (2%)
    pallas_call x1, Pallas kernels, fused(): pl.pallas_call(lambda *refs: fused_kernel(nt, nm, nz, *refs), out_shape=j...  28 us
    broadcast_in_dim x1, other arithmetic, fused(): return result[None, None]  2.27 us
    unnamed x2, local copies, waits for them, and re-layouts  0.68 us

profile of v3, /device:TPU:0, one launch (start us, length us, event | category | flops | bytes accessed | tf_op | source)
XLA Modules:
  0.0 31.1 jit_solution(12955439896827316183)
XLA Ops:
  0.0 0.0 copy-start
  0.0 0.7 %copy-done = s32[4,4]{1,0:T(4,128)S(1)} copy-done((s32[4,4]{1,0:T(4,128)S(1)}, s32[4,4]{1,0:T(4,128)}, u32[]{:S(2)}) %copy-start) | copy-done | bytes 88
  0.7 0.1 compare_reduce_fusion
  0.8 28.0 %shard_map.64 = bf16[4,128,1024]{2,1,0:T(8,128)(2,1)} custom-call(bf16[512,1024]{1,0:T(8,128)(2,1)} %bitcast.6, f32[1,512]{1,0:T(1,128)} %bitcast.7, s32[4]{0:T(128)} %refs_2_.1, s32[8]{0:T(128)} %refs_3_.1, f32[4,8]{1,0:T(4,128)} %refs_4_.1), custom_call_target="tpu_custom_call" | custom-call | tf_op jit(solution)/shard_map/pallas_call | solution.py:354
  28.8 2.3 %select_bitcast_fusion = bf16[1,1,4,128,1024]{4,3,2,1,0:T(8,128)(2,1)} fusion(bf16[4,128,1024]{2,1,0:T(8,128)(2,1)} %shard_map.64, pred[1024]{0:T(1024)(128)(4,1)S(1)} %pad_add_fusion), kind=kLoop, calls=%fused_computation | loop fusion | flops 524288 | bytes 2098176 | tf_op jit(solution)/shard_map/broadcast_in_dim | solution.py:380
  (3 shorter events, 0.0 us)
Async XLA Ops:
  0.0 0.7 %copy-start = (s32[4,4]{1,0:T(4,128)S(1)}, s32[4,4]{1,0:T(4,128)}, u32[]{:S(2)}) copy-start(s32[4,4]{1,0:T(4,128)} %param.11) | copy-start | bytes 196

commit v4 on v3

--- a/solution.py
+++ b/solution.py
@@ -13,7 +13,7 @@
 
 
 def fused_kernel(
-    nt, nm, nz, g_ref, gam_ref, shift_ref, off_ref, coup_ref, out_ref,
+    nt, nm, nz, g_ref, gam_ref, shift_ref, off_ref, coup_ref, nbr_ref, out_ref,
     left, stage, cross, diag, held, fin, parts, tab,
     a_send, a_recv, z_send, z_recv, f_send, f_recv, own_sem,
 ):
@@ -267,18 +267,27 @@
             if kk > 0:
                 near_copy(u, kk, who).wait_recv()
 
+    def kept(tile):
+        found = jnp.float32(0.0)
+        for b in range(nbr_ref.shape[1]):
+            found = jnp.where(nbr_ref[t, b] == tile, 1.0, found)
+        return found
+
     def store(part, tile, flip):
+        keep = kept(tile)
+
         @pl.loop(0, nt)
         def _(e):
-            re, im = parts[part, e, :, :tall], parts[part, e, :, tall:]
+            re, im = parts[part, e, :, :tall].astype(jnp.float32), parts[part, e, :, tall:].astype(jnp.float32)
             if flip:
-                re = re.astype(jnp.float32).T.astype(jnp.bfloat16)
-                im = (-(im.astype(jnp.float32).T)).astype(jnp.bfloat16)
+                re, im = re.T, -im.T
+            re, im = (re * keep).astype(jnp.bfloat16), (im * keep).astype(jnp.bfloat16)
             out_ref[e, :, pl.ds(pl.multiple_of(tile * tall, tall), tall)] = re
             out_ref[e, :, pl.ds(pl.multiple_of(orb + tile * tall, tall), tall)] = im
 
     def store_diagonal():
         row, col = triangle()
+        keep = kept(t)
 
         @pl.loop(0, nt)
         def _(e):
@@ -289,8 +298,8 @@
             turned = both.T
             re = jnp.where(row > col, turned, both)
             im = jnp.where(row > col, both, jnp.where(row < col, -turned, 0.0))
-            out_ref[e, :, pl.ds(pl.multiple_of(t * tall, tall), tall)] = re.astype(jnp.bfloat16)
-            out_ref[e, :, pl.ds(pl.multiple_of(orb + t * tall, tall), tall)] = im.astype(jnp.bfloat16)
+            out_ref[e, :, pl.ds(pl.multiple_of(t * tall, tall), tall)] = (re * keep).astype(jnp.bfloat16)
+            out_ref[e, :, pl.ds(pl.multiple_of(orb + t * tall, tall), tall)] = (im * keep).astype(jnp.bfloat16)
 
     forward(2)
     mix(0)
@@ -332,14 +341,6 @@
             @pl.when(has_down)
             def _():
                 z_copy(u, i, j, False).wait_send()
-
-
-def column_mask(tile_nbr, orbitals, per_tile):
-    tile_here = lax.axis_index("tile")
-    neighbours = lax.dynamic_index_in_dim(tile_nbr, tile_here, 0, keepdims=False)
-    coltile = jnp.arange(orbitals, dtype=jnp.int32) // per_tile
-    colmask = jnp.any(coltile[:, None] == neighbours[None, :], axis=1)
-    return jnp.concatenate([colmask, colmask])
 
 
 def fused(green_ret, injection, mom_shift, phon_off, coupling, tile_nbr):
@@ -354,7 +355,7 @@
     total = pl.pallas_call(
         lambda *refs: fused_kernel(nt, nm, nz, *refs),
         out_shape=jax.ShapeDtypeStruct((nt, tall, width), jnp.bfloat16),
-        in_specs=[vmem, vmem, smem, smem, smem],
+        in_specs=[vmem, vmem, smem, smem, smem, smem],
         out_specs=vmem,
         scratch_shapes=[
             pltpu.VMEM((nt, 2 * tall, width), jnp.bfloat16),
@@ -374,10 +375,8 @@
             dma((4,)),
         ],
         compiler_params=pltpu.CompilerParams(collective_id=0, has_side_effects=True),
-    )(green, gamma, mom_shift, phon_off, coupling)
-    colmask = column_mask(tile_nbr, orbitals, tall)
-    result = jnp.where(colmask[None, None, :], total, jnp.zeros((), jnp.bfloat16))
-    return result[None, None]
+    )(green, gamma, mom_shift, phon_off, coupling, tile_nbr)
+    return total[None, None]
 
 
 def with_halo(shard, sides, width):

time: 31.4 us -> 30.5 us (0.971)
  other arithmetic: 2.37 us -> 0 us
  local copies, waits for them, and re-layouts: 0.69 us -> 2.26 us
    broadcast_in_dim x1 -> x0, other arithmetic: 2.27 us -> none  [fused(): return result[None, None]]
    unnamed x2 -> x1, local copies, waits for them, and re-layouts: 0.68 us -> 2.26 us
where the time goes in v4:
time: 30.5 us; the launch traced here: 30.3 us
  Pallas kernels  28 us (92%)
  local copies, waits for them, and re-layouts  2.26 us (7%)
    pallas_call x1, Pallas kernels, fused(): pl.pallas_call(lambda *refs: fused_kernel(nt, nm, nz, *refs), out_shape=j...  28 us
    unnamed x1, local copies, waits for them, and re-layouts  2.26 us

profile of v4, /device:TPU:0, one launch (start us, length us, event | category | flops | bytes accessed | tf_op | source)
XLA Modules:
  0.0 30.3 jit_solution(1227131597071185509)
XLA Ops:
  0.0 28.0 %shard_map.64 = bf16[4,128,1024]{2,1,0:T(8,128)(2,1)} custom-call(bf16[512,1024]{1,0:T(8,128)(2,1)} %bitcast.4, f32[1,512]{1,0:T(1,128)} %bitcast.5, s32[4]{0:T(128)} %refs_2_.1, s32[8]{0:T(128)} %refs_3_.1, f32[4,8]{1,0:T(4,128)} %refs_4_.1, s32[4,4]{1,0:T(4,128)} %refs_5_.1), custom_call_target="tpu_custom_call" | custom-call | tf_op jit(solution)/shard_map/pallas_call | solution.py:355
  28.0 2.3 %copy.8 = bf16[1,1,4,128,1024]{4,3,2,1,0:T(8,128)(2,1)} copy(bf16[1,1,4,128,1024]{4,3,2,1,0:T(8,128)(2,1)} %bitcast.3) | data formatting | bytes 2097152
